TPU v7x, 256 devices: a whole 4x4x8 slice. The times are simulated.
256 devices in a mesh: context: 8 (over y, x_lo), tensor: 8 (over z), fsdp: 4 (over x_hi, core).
Axes of the slice: x: 4 (x_hi: 2, x_lo: 2; x = x_hi * 2 + x_lo), y: 4, z: 8, core: 2. Of those that a mesh axis runs over, the one named last changes fastest.
Arguments:
- queries: bfloat16 [4, 1024, 4096], P('fsdp', 'context', 'tensor'), may hold values from -8 to 8
- keys: bfloat16 [4, 1024, 4096], P('fsdp', 'context', 'tensor'), may hold values from -8 to 8
- values: bfloat16 [4, 1024, 4096], P('fsdp', 'context', 'tensor'), may hold values from -6 to 6
- out_grad: bfloat16 [4, 1024, 4096], P('fsdp', 'context', 'tensor'), may hold values from -6 to 6
- out_weight: bfloat16 [4096, 4096], P('fsdp', 'tensor'), may hold values from -0.09375 to 0.09375
- slopes: float32 [32], P('tensor'), may hold values from 0.00012207031 to 0.05
- counts: int32 [4, 8], P('fsdp', 'context'), may hold values from 1 to 128, 640 in all within a row
- gaps: int32 [4, 1024], P('fsdp', 'context'), may hold values from 1 to 12
Outputs:
- query_grad: bfloat16 [4, 1024, 4096], P('fsdp', 'context', 'tensor')
- key_grad: bfloat16 [4, 1024, 4096], P('fsdp', 'context', 'tensor')
- value_grad: bfloat16 [4, 1024, 4096], P('fsdp', 'context', 'tensor')
- weight_grad: float32 [4096, 4096], P('fsdp', 'tensor')
Inputs may be any that keep to these rules, and one draw needn't show every extreme that they name: In each sequence the counts sum to 640 and the largest is 128.
All inputs are finite; a program needn't handle non-finite values. No bound on the sum of `counts` on one device may be relied on, other than what follows from the above.
Results may differ from a plain program's by a relative error of at most 0.022.
Values may be sent and summed in bfloat16 or wider, within the bound.
A program may use at most 64 MiB of HBM per device.

v0:
```python
import jax
import jax.numpy as jnp
from jax import lax
from jax.sharding import PartitionSpec as P

NEG = -1e30


def laid_out(tiles, dim):
    lengths = list(tiles.shape[1:])
    lengths[dim] *= tiles.shape[0]
    return jnp.moveaxis(tiles, 0, dim).reshape(lengths)


def gather_together(arrays, axis, dims):
    flat = jnp.concatenate([a.reshape(-1) for a in arrays])
    lines, at, finished = (lax.all_gather(flat, axis), 0, [])
    for a, dim in zip(arrays, dims):
        tiles = lines[:, at : at + a.size].reshape(-1, *a.shape)
        finished.append(laid_out(tiles, dim))
        at += a.size
    return tuple(finished)


def copy_for_each(x, axis):
    count = lax.axis_size(axis)
    return lax.all_to_all(jnp.broadcast_to(x[None], (count, *x.shape)), axis, 0, 0, tiled=True)


def collect(x, axis, dim):
    tiles = copy_for_each(x, axis)
    return laid_out(tiles, dim)


def in_one_piece(arrays, axis, dim, along):
    both = jnp.concatenate(arrays, axis=along)
    result, at, finished = (lax.all_gather(both, axis, axis=dim, tiled=True), 0, [])
    for a in arrays:
        finished.append(lax.slice_in_dim(result, at, at + a.shape[along], axis=along))
        at += a.shape[along]
    return tuple(finished)


def per_device(queries, keys, values, out_grad, out_weight, slopes, counts, gaps):
    row_count = queries.shape[1]
    width = queries.shape[2]
    head_count = slopes.shape[0]
    head_size = width // head_count
    scaling = head_size ** (-0.5)
    shard_count = lax.axis_size("context")
    my_start = lax.axis_index("context") * row_count
    total_slots = shard_count * row_count
    all_gaps, all_counts = gather_together((gaps, counts), "context", (1, 1))
    slot_index = jnp.arange(total_slots, dtype=jnp.int32)
    owner = slot_index // row_count
    shard_ids = jnp.arange(shard_count, dtype=jnp.int32)
    slot_limit = jnp.sum(
        jnp.where(owner[:, None] == shard_ids[None, :], all_counts[0][None, :], 0), axis=1
    )
    slot_valid = slot_index % row_count < slot_limit
    offsets = jnp.cumsum(jnp.where(slot_valid, all_gaps[0], 0)).astype(jnp.float32)
    my_valid = lax.dynamic_slice_in_dim(slot_valid, my_start, row_count)
    grad_full = collect(out_grad[0], "tensor", 1)
    grad_masked = jnp.where(my_valid[:, None], grad_full, jnp.zeros_like(grad_full))
    columns = grad_masked
    grad_heads = jnp.dot(
        columns,
        lax.all_gather(out_weight, "fsdp", axis=0, tiled=True),
        preferred_element_type=jnp.float32,
    ).astype(jnp.bfloat16)
    local_q = queries[0]
    local_k = keys[0]
    local_v = values[0]
    key_full, value_full = in_one_piece((local_k, local_v), "context", 0, 1)

    def split(block):
        return block.reshape(block.shape[0], head_count, head_size)

    def scores(q_block, q_start, k_block, k_start):
        query_count = q_block.shape[0]
        key_count = k_block.shape[0]
        logits = (
            jnp.einsum(
                "qhd,khd->hqk", split(q_block), split(k_block), preferred_element_type=jnp.float32
            )
            * scaling
        )
        q_offset = lax.dynamic_slice_in_dim(offsets, q_start, query_count)
        k_offset = lax.dynamic_slice_in_dim(offsets, k_start, key_count)
        k_valid = lax.dynamic_slice_in_dim(slot_valid, k_start, key_count)
        q_slot = q_start + jnp.arange(query_count, dtype=jnp.int32)
        k_slot = k_start + jnp.arange(key_count, dtype=jnp.int32)
        allowed = k_valid[None, :] & (k_slot[None, :] <= q_slot[:, None])
        logits = logits - slopes[:, None, None] * (
            q_offset[None, :, None] - k_offset[None, None, :]
        )
        return (jnp.where(allowed[None], logits, NEG), allowed)

    def visit(needed, work, carry):
        return lax.cond(needed, work, lambda held: held, carry)

    def tile_terms(q_block, g_block, q_lse, q_delta, q_start, k_block, v_block, k_start):
        logits, allowed = scores(q_block, q_start, k_block, k_start)
        probs = jnp.where(allowed[None], jnp.exp(logits - q_lse[:, :, None]), 0.0)
        value_dots = jnp.einsum(
            "qhd,khd->hqk", split(g_block), split(v_block), preferred_element_type=jnp.float32
        )
        dscore = (probs * (value_dots - q_delta[:, :, None])).astype(jnp.bfloat16)
        return (probs.astype(jnp.bfloat16), dscore)

    block = 2 * row_count
    block_total = total_slots // block
    my_last = my_start + row_count - 1

    def mass_step(block_index, carry):
        k_start = block_index * block
        k_block = lax.dynamic_slice_in_dim(key_full, k_start, block, 0)

        def work(state):
            peak, mass = state
            logits, allowed = scores(local_q, my_start, k_block, k_start)
            new_peak = jnp.maximum(peak, jnp.max(logits, axis=2))
            weights = jnp.where(allowed[None], jnp.exp(logits - new_peak[:, :, None]), 0.0)
            return (new_peak, mass * jnp.exp(peak - new_peak) + jnp.sum(weights, axis=2))

        return visit(k_start <= my_last, work, carry)

    start_state = (
        jnp.full((head_count, row_count), NEG, jnp.float32),
        jnp.zeros((head_count, row_count), jnp.float32),
    )
    peak, mass = lax.fori_loop(0, block_total, mass_step, start_state)
    log_total = peak + jnp.log(mass)

    def output_step(block_index, carry):
        k_start = block_index * block
        k_block = lax.dynamic_slice_in_dim(key_full, k_start, block, 0)
        v_block = lax.dynamic_slice_in_dim(value_full, k_start, block, 0)

        def work(acc):
            logits, allowed = scores(local_q, my_start, k_block, k_start)
            probs_b = jnp.where(allowed[None], jnp.exp(logits - log_total[:, :, None]), 0.0).astype(
                jnp.bfloat16
            )
            return acc + jnp.einsum(
                "hqk,khd->qhd", probs_b, split(v_block), preferred_element_type=jnp.float32
            ).reshape(row_count, width)

        return visit(k_start <= my_last, work, carry)

    output_b = lax.fori_loop(
        0, block_total, output_step, jnp.zeros((row_count, width), jnp.float32)
    ).astype(jnp.bfloat16)
    delta = jnp.sum(
        (grad_heads.astype(jnp.float32) * output_b.astype(jnp.float32)).reshape(
            row_count, head_count, head_size
        ),
        axis=2,
    ).T

    def query_step(block_index, carry):
        k_start = block_index * block
        k_block = lax.dynamic_slice_in_dim(key_full, k_start, block, 0)
        v_block = lax.dynamic_slice_in_dim(value_full, k_start, block, 0)

        def work(acc):
            probs_b, dscore = tile_terms(
                local_q, grad_heads, log_total, delta, my_start, k_block, v_block, k_start
            )
            return (
                acc
                + jnp.einsum(
                    "hqk,khd->qhd", dscore, split(k_block), preferred_element_type=jnp.float32
                ).reshape(row_count, width)
                * scaling
            )

        return visit(k_start <= my_last, work, carry)

    query_grad = lax.fori_loop(
        0, block_total, query_step, jnp.zeros((row_count, width), jnp.float32)
    ).astype(jnp.bfloat16)
    stats_lse, stats_delta = in_one_piece((log_total, delta), "context", 1, 0)
    start = jnp.int32(0)
    q_piece, g_piece = in_one_piece((local_q, grad_heads), "context", 0, 1)
    piece_rows = q_piece.shape[0]

    def work(held):
        probs_b, dscore = tile_terms(
            q_piece, g_piece, stats_lse, stats_delta, start, local_k, local_v, my_start
        )
        key_part = (
            jnp.einsum(
                "hqk,qhd->khd", dscore, split(q_piece), preferred_element_type=jnp.float32
            ).reshape(row_count, width)
            * scaling
        )
        value_part = jnp.einsum(
            "hqk,qhd->khd", probs_b, split(g_piece), preferred_element_type=jnp.float32
        ).reshape(row_count, width)
        return jnp.concatenate([key_part, value_part], axis=1)

    key_value_grads = visit(
        start + piece_rows - 1 >= my_start, work, jnp.zeros((row_count, 2 * width), jnp.float32)
    )
    key_grad = key_value_grads[:, :width].astype(jnp.bfloat16)
    value_grad = key_value_grads[:, width:].astype(jnp.bfloat16)
    columns = grad_masked
    weight_share = lax.psum_scatter(
        lax.dot_general(
            columns, output_b, (((0,), (0,)), ((), ())), preferred_element_type=jnp.float32
        ),
        "fsdp",
        scatter_dimension=0,
        tiled=True,
    )
    weight_grad = lax.psum(weight_share, "context")
    return (query_grad[None], key_grad[None], value_grad[None], weight_grad)


def solution(mesh):
    placed = (
        P("fsdp", "context", "tensor"),
        P("fsdp", "context", "tensor"),
        P("fsdp", "context", "tensor"),
        P("fsdp", "context", "tensor"),
        P("fsdp", "tensor"),
        P("tensor"),
        P("fsdp", "context"),
        P("fsdp", "context"),
    )
    return jax.shard_map(
        per_device,
        mesh=mesh,
        in_specs=placed,
        out_specs=(
            P("fsdp", "context", "tensor"),
            P("fsdp", "context", "tensor"),
            P("fsdp", "context", "tensor"),
            P("fsdp", "tensor"),
        ),
        check_vma=False,
    )
```

profile of v0, /device:TPU:1, one launch (start us, length us, event | category | flops | bytes accessed | tf_op | source)
XLA Modules:
  0.0 374.7 jit_solution(449688491105010853)
XLA Ops:
  7.2 1.1 copy.161
  8.3 1.0 copy.162
  9.3 0.7 pad_maximum_fusion.1
  10.1 0.7 all-gather.7.cloned.1.call-update
  10.9 1.1 broadcast_in_dim.191
  11.9 9.0 %all-to-all-start = ((bf16[8,128,512]{2,1,0:T(8,128)(2,1)}), bf16[8,128,512]{2,1,0:T(8,128)(2,1)S(1)}, u32[]{:S(2)}, u32[]{:S(2)}) async-start(bf16[8,128,512]{2,1,0:T(8,128)(2,1)} %broadcast_in_dim.191), calls=%async_computation | async-start | bytes 2097152 | tf_op jit(solution)/shard_map/all_to_all | solution.py:27
  21.6 0.6 dynamic-slice
  22.9 0.1 add_dynamic-update-slice_fusion
  23.0 10.2 %all-reduce = s32[1032]{0:T(1024)S(1)} all-reduce(s32[1032]{0:T(1024)S(1)} %add_dynamic-update-slice_fusion), channel_id=2, replica_groups=mesh['context'=8,'tensor'=8,'fsdp'=4] {'context'}, use_global_device_ids=true, to_apply=%add | all-reduce | flops 1032 | bytes 8256
  33.2 0.1 reshape.459
  33.3 0.1 slice_reduce_fusion.1
  33.4 0.1 select_reduce_fusion.1
  33.5 0.3 reduce-window.9
  33.9 0.1 dynamic_slice.124
  34.0 0.1 slice_reduce_fusion
  34.2 15.9 %all-to-all-done = bf16[8,128,512]{2,1,0:T(8,128)(2,1)S(1)} async-done(((bf16[8,128,512]{2,1,0:T(8,128)(2,1)}), bf16[8,128,512]{2,1,0:T(8,128)(2,1)S(1)}, u32[]{:S(2)}, u32[]{:S(2)}) %all-to-all-start) | async-done | bytes 1048608 | tf_op jit(solution)/shard_map/all_to_all | solution.py:27
  50.1 0.7 copy.163
  50.8 0.1 bitcast_select_fusion
  50.9 14.5 %all-gather.5.cloned.1.call-done = bf16[1024,1024]{0,1:T(8,128)(2,1)} async-done(((bf16[128,1024]{0,1:T(8,128)(2,1)}), bf16[1024,1024]{0,1:T(8,128)(2,1)}) %all-gather.5.cloned.1.call-update) | async-done | bytes 2097168 | tf_op jit(solution)/shard_map/all_gather | solution.py:37
  65.4 2.7 fusion.64
  68.1 1.2 while.47
  68.1 1.0 conditional.8
  68.4 0.1 compare_and_fusion
  68.6 0.1 broadcast_subtract_fusion
  68.7 0.3 fusion.61
  69.0 0.1 select_reduce_fusion
  69.4 3.6 while.48
  69.4 3.5 conditional.9
  69.6 1.0 constant_dynamic-slice_fusion.1
  70.6 0.8 compare_and_fusion.1
  71.4 0.1 broadcast_subtract_fusion.1
  71.5 1.3 fusion.11
  73.0 0.1 copy.164
  73.1 4.5 %fusion.65 = f32[4096,512]{1,0:T(8,128)} fusion(bf16[128,4096]{0,1:T(8,128)(2,1)S(1)} %bitcast_select_fusion, bf16[128,512]{1,0:T(8,128)(2,1)S(1)} %copy.164), kind=kOutput, calls=%fused_computation.117 | convolution fusion | flops 536870912 | bytes 9568256 | tf_op jit(solution)/shard_map/dot_general | solution.py:210
  77.7 35.0 %all-gather.7.cloned.1.call-done = bf16[4096,512]{1,0:T(8,128)(2,1)} async-done(((bf16[1024,512]{1,0:T(8,128)(2,1)}), bf16[4096,512]{1,0:T(8,128)(2,1)}) %all-gather.7.cloned.1.call-update) | async-done | bytes 4194320 | tf_op jit(solution)/shard_map/all_gather | solution.py:68
  112.6 2.9 convert_multiply_fusion
  115.6 0.8 pad_maximum_fusion.2
  116.4 81.4 %reduce-scatter.2.cloned.1.call-done = f32[1024,512]{1,0:T(8,128)} async-done(((f32[4096,512]{1,0:T(8,128)}), f32[1024,512]{1,0:T(8,128)}) %reduce-scatter.2.cloned.1.call-update) | async-done | bytes 2097168 | tf_op jit(solution)/shard_map/reduce_scatter | solution.py:209
  197.9 0.1 reshape.458
  198.0 0.2 reduce_sum.33
  198.3 2.5 while.49
  198.3 2.4 conditional.10
  198.6 1.0 constant_dynamic-slice_fusion.3
  199.6 0.1 compare_and_fusion.2
  199.7 0.1 broadcast_subtract_fusion.2
  199.9 0.3 fusion.32
  200.2 0.4 fusion.35
  200.8 0.8 copy.166
  201.6 31.4 %all_gather.23 = f32[8,1024]{1,0:T(8,128)S(1)} all-gather(f32[8,128]{1,0:T(8,128)S(1)} %pad_maximum_fusion.3), channel_id=1, replica_groups=mesh['context'=8,'tensor'=8,'fsdp'=4] {'context'}, dimensions={1}, use_global_device_ids=true | all-gather | bytes 36864 | tf_op jit(solution)/shard_map/all_gather | solution.py:37
  233.1 20.6 %all-gather.9.cloned.1.call-done = bf16[1024,1024]{1,0:T(8,128)(2,1)} async-done(((bf16[128,1024]{1,0:T(8,128)(2,1)}), bf16[1024,1024]{1,0:T(8,128)(2,1)}) %all-gather.9.cloned.1.call-update) | async-done | bytes 2097168 | tf_op jit(solution)/shard_map/all_gather | solution.py:37
  253.6 10.6 %conditional.4 = (bf16[128,1024]{0,1:T(8,128)(2,1)S(1)}) conditional(s32[]{:T(128)} %convert_element_type.72, () %tuple.110, (s32[]{:T(128)}, pred[1024]{0:T(1024)(128)(4,1)S(1)}, bf16[1024,1024]{1,0:T(8,128)(2,1)}, bf16[1,128,512]{2,1,0:T(8,128)(2,1)S(1)}, f32[4]{0:T(128)S(1)}, /*index=5*/f32[1024]{0:T(1024)S(1)}, f32[8,1024]{1,0:T(8,128)S(1)}, ...), branch_computations={%region_18.19_spmd, %region_19.20_spmd} | conditional | flops 543162496 | bytes 28286098 | solution.py:100
  253.8 0.6 fusion.63
  254.4 0.1 fusion.47
  254.6 1.0 broadcast_subtract_fusion.3
  255.6 2.9 copy.168
  258.5 0.2 fusion.62
  258.7 1.0 copy-done.1
  259.7 1.8 exponential_select_fusion
  261.5 2.3 fusion.43
  263.8 0.4 fusion.44
  264.3 0.1 copy.169
  264.4 0.7 slice_bitcast_fusion
  265.1 100.0 %all-reduce.3.cloned.1.call-done = f32[1024,512]{1,0:T(8,128)} async-done(((f32[1024,512]{1,0:T(8,128)}), f32[1024,512]{1,0:T(8,128)}) %all-reduce.3.cloned.1.call-update) | async-done | bytes 2097168 | tf_op jit(solution)/shard_map/psum | solution.py:217
  365.1 3.1 copy.235
  (85 shorter events, 2.0 us)
Async XLA Ops:
  7.2 3.7 copy-start.5
  7.2 58.2 %all-gather.5.cloned.1.call-start = ((), (), s32[]{:S(2)}) async-start(), calls=%async_computation.2 | async-start | bytes 2359296 | tf_op jit(solution)/shard_map/all_gather | solution.py:37
  10.1 11.6 %copy-start.11 = (u32[256]{0:T(256)S(1)}, u32[256]{0:T(256)}, u32[]{:S(2)}) copy-start(u32[256]{0:T(256)} %constant.260) | copy-start | bytes 3076
  10.1 12.8 %copy-start.8 = (s32[1,128]{1,0:T(1,128)S(1)}, s32[1,128]{1,0:T(1,128)}, u32[]{:S(2)}) copy-start(s32[1,128]{1,0:T(1,128)} %param.29) | copy-start | bytes 1540
  10.1 102.5 %all-gather.7.cloned.1.call-start = ((), (), s32[]{:S(2)}) async-start(), calls=%async_computation.3 | async-start | bytes 5242880 | tf_op jit(solution)/shard_map/all_gather | solution.py:68
  11.9 38.2 %all-to-all-start = ((bf16[8,128,512]{2,1,0:T(8,128)(2,1)}), bf16[8,128,512]{2,1,0:T(8,128)(2,1)S(1)}, u32[]{:S(2)}, u32[]{:S(2)}) async-start(bf16[8,128,512]{2,1,0:T(8,128)(2,1)} %broadcast_in_dim.191), calls=%async_computation | async-start | bytes 2097152 | tf_op jit(solution)/shard_map/all_to_all | solution.py:27
  20.9 176.9 %reduce-scatter.2.cloned.1.call-start = ((), (), s32[]{:S(2)}) async-start(), calls=%async_computation.5 | async-start | bytes 10485760 | tf_op jit(solution)/shard_map/reduce_scatter | solution.py:209
  50.9 17.2 %copy-start = (bf16[1,128,512]{2,1,0:T(8,128)(2,1)S(1)}, bf16[1,128,512]{2,1,0:T(8,128)(2,1)}, u32[]{:S(2)}) copy-start(bf16[1,128,512]{2,1,0:T(8,128)(2,1)} %param.22) | copy-start | bytes 393220
  50.9 17.2 %copy-start.9 = (f32[4]{0:T(128)S(1)}, f32[4]{0:T(128)}, u32[]{:S(2)}) copy-start(f32[4]{0:T(128)} %param.27) | copy-start | bytes 52
  77.6 176.0 %all-gather.9.cloned.1.call-start = ((), (), s32[]{:S(2)}) async-start(), calls=%async_computation.4 | async-start | bytes 2359296 | tf_op jit(solution)/shard_map/all_gather | solution.py:37
  116.3 248.8 %all-reduce.3.cloned.1.call-start = ((), (), s32[]{:S(2)}) async-start(), calls=%async_computation.6 | async-start | bytes 4194304 | tf_op jit(solution)/shard_map/psum | solution.py:217
  198.3 55.4 %copy-start.3 = (bf16[1,128,512]{2,1,0:T(8,128)(2,1)S(1)}, bf16[1,128,512]{2,1,0:T(8,128)(2,1)}, u32[]{:S(2)}) copy-start(bf16[1,128,512]{2,1,0:T(8,128)(2,1)} %param.24) | copy-start | bytes 393220
  198.3 55.4 %copy-start.4 = (bf16[1,128,512]{2,1,0:T(8,128)(2,1)S(1)}, bf16[1,128,512]{2,1,0:T(8,128)(2,1)}, u32[]{:S(2)}) copy-start(bf16[1,128,512]{2,1,0:T(8,128)(2,1)} %param.23) | copy-start | bytes 393220
  253.6 4.8 %copy-start.10 = (f32[4]{0:T(128)}, f32[4]{0:T(128)S(1)}, u32[]{:S(2)}) copy-start(f32[4]{0:T(128)S(1)} %get-tuple-element.954) | copy-start | bytes 52 | tf_op jit(solution)/shard_map/cond
  258.5 1.2 copy-start.2
  258.5 1.2 copy-start.7
  258.7 1.0 copy-start.1
  259.7 1.8 copy-start.6
Sparse Core Ops, SparseCore 0:
  10.2 55.1 all-gather.4
  67.2 45.3 all-gather.6
  115.5 82.3 reduce-scatter.1
  199.5 54.1 all-gather.8
  256.1 108.9 all-reduce.2
where the time goes:
time: 376 us; the launch traced here: 375 us
  waiting for transfers between devices  268 us (71%)
  blocking collectives  41.6 us (11%)
  local copies, waits for them, and re-layouts  20.3 us (5%)
  between operations  15.3 us (4%)
  matrix products  14.3 us (4%)
  starting transfers between devices  9.2 us (2%)
  other arithmetic  5.15 us (1%)
    psum x1, waiting for transfers between devices, per_device(): weight_grad = lax.psum(weight_share, 'context')  100 us
    reduce_scatter x1, waiting for transfers between devices, per_device(): lax.psum_scatter(lax.dot_general(columns, output_b, (((0,), (0,)), ((), (...  81.4 us
    all_gather x2, waiting for transfers between devices, in_one_piece(): lax.all_gather(both, axis, axis=dim, tiled=True)  35 us
    all_gather x1, waiting for transfers between devices, per_device(): lax.all_gather(out_weight, 'fsdp', axis=0, tiled=True)  35 us
    all_gather x1, blocking collectives, in_one_piece(): lax.all_gather(both, axis, axis=dim, tiled=True)  31.4 us
    all_to_all x1, waiting for transfers between devices, copy_for_each(): lax.all_to_all(jnp.broadcast_to(x[None], (count, *x.shape)), axis, 0, 0,...  15.9 us
    unnamed x1, blocking collectives  10.2 us
    all_to_all x1, starting transfers between devices, copy_for_each(): lax.all_to_all(jnp.broadcast_to(x[None], (count, *x.shape)), axis, 0, 0,...  9 us
  transfers between devices with their start and end apart: 6, of which 6 were waited for; matrix products, arithmetic and copies ran while one was open for 9% of the time, Pallas kernels for 0%

commit v1 on v0

--- a/solution.py
+++ b/solution.py
@@ -214,7 +214,7 @@
         scatter_dimension=0,
         tiled=True,
     )
-    weight_grad = lax.psum(weight_share, "context")
+    weight_grad = jnp.sum(lax.all_gather(weight_share, "context"), axis=0)
     return (query_grad[None], key_grad[None], value_grad[None], weight_grad)
 
 

time: 376 us -> 600 us (1.60)
  waiting for transfers between devices: 268 us -> 481 us
  other arithmetic: 5.15 us -> 15.4 us
    all_gather x0 -> x1, waiting for transfers between devices: none -> 315 us  [per_device(): weight_grad = jnp.sum(lax.all_gather(weight_share, 'context'), axis=0)]
    psum x1 -> x0, waiting for transfers between devices: 100 us -> none  [per_device(): weight_grad = lax.psum(weight_share, 'context')]
    reduce_sum x0 -> x1, other arithmetic: none -> 9.4 us  [per_device(): weight_grad = jnp.sum(lax.all_gather(weight_share, 'context'), axis=0)]
  transfers between devices with their start and end apart: 6 -> 6, of which waited for: 6 -> 6; matrix products, arithmetic and copies ran while one was open for 9% -> 6% of each run, Pallas kernels for 0% -> 0%
where the time goes in v1:
time: 600 us; the launch traced here: 599 us
  waiting for transfers between devices  481 us (80%)
  blocking collectives  43.1 us (7%)
  local copies, waits for them, and re-layouts  17.9 us (3%)
  matrix products  16.3 us (3%)
  other arithmetic  15.4 us (3%)
  between operations  15.3 us (3%)
  starting transfers between devices  9.2 us (2%)
    all_gather x1, waiting for transfers between devices, per_device(): weight_grad = jnp.sum(lax.all_gather(weight_share, 'context'), axis=0)  315 us
    reduce_scatter x1, waiting for transfers between devices, per_device(): lax.psum_scatter(lax.dot_general(columns, output_b, (((0,), (0,)), ((), (...  81.6 us
    all_gather x1, waiting for transfers between devices, per_device(): lax.all_gather(out_weight, 'fsdp', axis=0, tiled=True)  34.9 us
    all_gather x2, waiting for transfers between devices, in_one_piece(): lax.all_gather(both, axis, axis=dim, tiled=True)  33.6 us
    all_gather x1, blocking collectives, in_one_piece(): lax.all_gather(both, axis, axis=dim, tiled=True)  32.9 us
    all_to_all x1, waiting for transfers between devices, copy_for_each(): lax.all_to_all(jnp.broadcast_to(x[None], (count, *x.shape)), axis, 0, 0,...  15.9 us
  transfers between devices with their start and end apart: 6, of which 6 were waited for; matrix products, arithmetic and copies ran while one was open for 6% of the time, Pallas kernels for 0%

profile of v1, /device:TPU:1, one launch (start us, length us, event | category | flops | bytes accessed | tf_op | source)
XLA Modules:
  0.0 599.3 jit_solution(18089130272076287807)
XLA Ops:
  7.2 1.1 copy.162
  8.3 1.0 copy.161
  9.3 0.7 pad_maximum_fusion.1
  10.1 0.7 all-gather.9.cloned.1.call-update
  10.9 1.1 broadcast_in_dim.191
  11.9 9.0 %all-to-all-start = ((bf16[8,128,512]{2,1,0:T(8,128)(2,1)}), bf16[8,128,512]{2,1,0:T(8,128)(2,1)S(1)}, u32[]{:S(2)}, u32[]{:S(2)}) async-start(bf16[8,128,512]{2,1,0:T(8,128)(2,1)} %broadcast_in_dim.191), calls=%async_computation | async-start | bytes 2097152 | tf_op jit(solution)/shard_map/all_to_all | solution.py:27
  21.6 0.7 dynamic-slice
  22.9 0.1 add_dynamic-update-slice_fusion
  23.1 10.2 %all-reduce = s32[1032]{0:T(1024)S(1)} all-reduce(s32[1032]{0:T(1024)S(1)} %add_dynamic-update-slice_fusion), channel_id=2, replica_groups=mesh['context'=8,'tensor'=8,'fsdp'=4] {'context'}, use_global_device_ids=true, to_apply=%add | all-reduce | flops 1032 | bytes 8256
  33.3 0.1 slice_reduce_fusion.1
  33.5 0.1 select_reduce_fusion.1
  33.6 0.3 reduce-window.9
  34.0 0.1 slice_reduce_fusion
  34.2 15.9 %all-to-all-done = bf16[8,128,512]{2,1,0:T(8,128)(2,1)S(1)} async-done(((bf16[8,128,512]{2,1,0:T(8,128)(2,1)}), bf16[8,128,512]{2,1,0:T(8,128)(2,1)S(1)}, u32[]{:S(2)}, u32[]{:S(2)}) %all-to-all-start) | async-done | bytes 1048608 | tf_op jit(solution)/shard_map/all_to_all | solution.py:27
  50.1 0.7 copy.163
  50.8 0.1 bitcast_select_fusion
  50.9 14.5 %all-gather.7.cloned.1.call-done = bf16[1024,1024]{0,1:T(8,128)(2,1)} async-done(((bf16[128,1024]{0,1:T(8,128)(2,1)}), bf16[1024,1024]{0,1:T(8,128)(2,1)}) %all-gather.7.cloned.1.call-update) | async-done | bytes 2097168 | tf_op jit(solution)/shard_map/all_gather | solution.py:37
  65.4 2.7 fusion.64
  68.1 1.2 while.47
  68.1 1.1 conditional.8
  68.3 0.1 broadcast_subtract_fusion
  68.6 0.1 compare_and_fusion
  68.7 0.3 fusion.61
  69.1 0.1 select_reduce_fusion
  69.4 3.7 while.48
  69.4 3.5 conditional.9
  69.4 1.0 constant_dynamic-slice_fusion.1
  70.6 0.1 broadcast_subtract_fusion.1
  70.7 0.1 dynamic_slice.111
  70.8 0.8 compare_and_fusion.1
  71.6 1.3 fusion.11
  73.0 0.1 copy.164
  73.2 4.5 fusion.65
  77.7 34.9 %all-gather.9.cloned.1.call-done = bf16[4096,512]{1,0:T(8,128)(2,1)} async-done(((bf16[1024,512]{1,0:T(8,128)(2,1)}), bf16[4096,512]{1,0:T(8,128)(2,1)}) %all-gather.9.cloned.1.call-update) | async-done | bytes 4194320 | tf_op jit(solution)/shard_map/all_gather | solution.py:68
  112.6 2.9 convert_multiply_fusion
  115.5 0.7 pad_maximum_fusion.2
  116.4 81.6 %reduce-scatter.2.cloned.1.call-done = f32[1024,512]{1,0:T(8,128)} async-done(((f32[4096,512]{1,0:T(8,128)}), f32[1024,512]{1,0:T(8,128)}) %reduce-scatter.2.cloned.1.call-update) | async-done | bytes 2097168 | tf_op jit(solution)/shard_map/reduce_scatter | solution.py:209
  197.9 0.1 reshape.458
  198.0 0.2 reduce_sum.42
  198.4 2.6 while.49
  198.4 2.4 conditional.10
  198.4 1.0 constant_dynamic-slice_fusion.3
  199.6 0.1 broadcast_subtract_fusion.2
  199.8 0.1 compare_and_fusion.2
  200.0 0.3 fusion.32
  200.3 0.4 fusion.35
  201.0 0.8 copy.166
  201.7 32.9 %all_gather.29 = f32[8,1024]{1,0:T(8,128)} all-gather(f32[8,128]{1,0:T(8,128)S(1)} %pad_maximum_fusion.3), channel_id=1, replica_groups=mesh['context'=8,'tensor'=8,'fsdp'=4] {'context'}, dimensions={1}, use_global_device_ids=true | all-gather | bytes 36864 | tf_op jit(solution)/shard_map/all_gather | solution.py:37
  234.7 19.1 %all-gather.11.cloned.1.call-done = bf16[1024,1024]{1,0:T(8,128)(2,1)} async-done(((bf16[128,1024]{1,0:T(8,128)(2,1)}), bf16[1024,1024]{1,0:T(8,128)(2,1)}) %all-gather.11.cloned.1.call-update) | async-done | bytes 2097168 | tf_op jit(solution)/shard_map/all_gather | solution.py:37
  253.8 14.2 %conditional.4 = (bf16[128,1024]{0,1:T(8,128)(2,1)S(1)}) conditional(s32[]{:T(128)} %convert_element_type.72, () %tuple.110, (s32[]{:T(128)}, pred[1024]{0:T(1024)(128)(4,1)S(1)}, bf16[1024,1024]{1,0:T(8,128)(2,1)}, bf16[1,128,512]{2,1,0:T(8,128)(2,1)}, f32[4]{0:T(128)S(1)}, /*index=5*/f32[1024]{0:T(1024)S(1)}, f32[8,1024]{1,0:T(8,128)}, ...), branch_computations={%region_18.19_spmd, %region_19.20_spmd} | conditional | flops 543162496 | bytes 23108662 | solution.py:100
  253.8 2.9 copy.168
  256.7 1.1 fusion.62
  257.8 0.6 fusion.63
  258.5 1.0 broadcast_subtract_fusion.3
  259.6 0.1 fusion.47
  259.7 0.7 reshape_squeeze.21
  260.4 2.4 exponential_select_fusion
  262.8 1.1 fusion.44
  264.0 3.0 fusion.43
  267.0 0.9 pad_maximum_fusion
  268.0 0.1 copy.169
  268.1 0.7 slice_bitcast_fusion
  268.8 314.5 %all-gather.13.cloned.1.call-done = f32[8192,512]{1,0:T(8,128)} async-done(((f32[1024,512]{1,0:T(8,128)}), f32[8192,512]{1,0:T(8,128)}) %all-gather.13.cloned.1.call-update) | async-done | bytes 16777232 | tf_op jit(solution)/shard_map/all_gather | solution.py:217
  583.3 9.4 %reduce_sum.43 = f32[1024,512]{1,0:T(8,128)} reduce(f32[8,1024,512]{2,1,0:T(8,128)} %bitcast.119, f32[]{:T(128)} %constant.239.clone.1), dimensions={0}, to_apply=%region_21.22 | reduce | flops 3670016 | bytes 18874372 | tf_op jit(solution)/shard_map/reduce_sum | solution.py:217
  (81 shorter events, 2.0 us)
Async XLA Ops:
  7.2 3.7 copy-start.4
  7.2 58.2 %all-gather.7.cloned.1.call-start = ((), (), s32[]{:S(2)}) async-start(), calls=%async_computation.2 | async-start | bytes 2359296 | tf_op jit(solution)/shard_map/all_gather | solution.py:37
  10.1 11.6 %copy-start.9 = (u32[256]{0:T(256)S(1)}, u32[256]{0:T(256)}, u32[]{:S(2)}) copy-start(u32[256]{0:T(256)} %constant.260) | copy-start | bytes 3076
  10.1 12.9 %copy-start.7 = (s32[1,128]{1,0:T(1,128)S(1)}, s32[1,128]{1,0:T(1,128)}, u32[]{:S(2)}) copy-start(s32[1,128]{1,0:T(1,128)} %param.29) | copy-start | bytes 1540
  10.1 102.5 %all-gather.9.cloned.1.call-start = ((), (), s32[]{:S(2)}) async-start(), calls=%async_computation.3 | async-start | bytes 5242880 | tf_op jit(solution)/shard_map/all_gather | solution.py:68
  11.9 38.2 %all-to-all-start = ((bf16[8,128,512]{2,1,0:T(8,128)(2,1)}), bf16[8,128,512]{2,1,0:T(8,128)(2,1)S(1)}, u32[]{:S(2)}, u32[]{:S(2)}) async-start(bf16[8,128,512]{2,1,0:T(8,128)(2,1)} %broadcast_in_dim.191), calls=%async_computation | async-start | bytes 2097152 | tf_op jit(solution)/shard_map/all_to_all | solution.py:27
  20.9 177.0 %reduce-scatter.2.cloned.1.call-start = ((), (), s32[]{:S(2)}) async-start(), calls=%async_computation.5 | async-start | bytes 10485760 | tf_op jit(solution)/shard_map/reduce_scatter | solution.py:209
  50.9 17.2 %copy-start = (bf16[1,128,512]{2,1,0:T(8,128)(2,1)S(1)}, bf16[1,128,512]{2,1,0:T(8,128)(2,1)}, u32[]{:S(2)}) copy-start(bf16[1,128,512]{2,1,0:T(8,128)(2,1)} %param.22) | copy-start | bytes 393220
  50.9 17.2 %copy-start.8 = (f32[4]{0:T(128)S(1)}, f32[4]{0:T(128)}, u32[]{:S(2)}) copy-start(f32[4]{0:T(128)} %param.27) | copy-start | bytes 52
  77.6 176.2 %all-gather.11.cloned.1.call-start = ((), (), s32[]{:S(2)}) async-start(), calls=%async_computation.4 | async-start | bytes 2359296 | tf_op jit(solution)/shard_map/all_gather | solution.py:37
  116.3 467.0 %all-gather.13.cloned.1.call-start = ((), (), s32[]{:S(2)}) async-start(), calls=%async_computation.6 | async-start | bytes 18874368 | tf_op jit(solution)/shard_map/all_gather | solution.py:217
  198.4 55.4 %copy-start.1 = (bf16[1,128,512]{2,1,0:T(8,128)(2,1)S(1)}, bf16[1,128,512]{2,1,0:T(8,128)(2,1)}, u32[]{:S(2)}) copy-start(bf16[1,128,512]{2,1,0:T(8,128)(2,1)} %param.24) | copy-start | bytes 393220
  256.6 1.2 copy-start.5
  256.7 3.0 copy-start.2
  262.8 1.1 copy-start.6
  264.0 3.1 copy-start.3
Sparse Core Ops, SparseCore 0:
  10.2 55.1 all-gather.6
  67.2 45.3 all-gather.8
  115.4 82.4 reduce-scatter.1
  199.6 54.1 all-gather.10
  255.4 327.8 all-gather.12
